TPU v7x, 512 devices: a whole 4x8x8 slice. The times are simulated.
512 devices in a mesh: seq: 64 (over y_hi, z, core), tp: 8 (over x, y_lo).
Axes of the slice: x: 4, y: 8 (y_hi: 4, y_lo: 2; y = y_hi * 2 + y_lo), z: 8, core: 2. Of those that a mesh axis runs over, the one named last changes fastest.
Arguments:
- frames_in: bfloat16 [1536, 32768], P('tp', 'seq'), may hold values from -30 to 30
- norm_gain: float32 [1536], P('tp'), may hold values from 0.5 to 2
- value_weight: bfloat16 [1536, 1536], P('tp'), may hold values from -0.15625 to 0.15625
- gate_weight: bfloat16 [1536, 1536], P('tp'), may hold values from -0.15625 to 0.15625
- depth_kernel: float32 [1536, 32], P('tp'), may hold values from -6 to 6
- conv_gain: float32 [1536], P('tp'), may hold values from 0.5 to 2
- out_weight: bfloat16 [1536, 1536], P('tp'), may hold values from -0.15625 to 0.15625
- cotangent: bfloat16 [1536, 32768], P('tp', 'seq'), may hold values from -15 to 15
Outputs:
- block_out: bfloat16 [1536, 32768], P('tp', 'seq')
- input_grad: bfloat16 [1536, 32768], P('tp', 'seq')
- grad_norm_gain: float32 [1536], P('tp')
- grad_value: bfloat16 [1536, 1536], P('tp')
- grad_gate: bfloat16 [1536, 1536], P('tp')
- grad_kernel: float32 [1536, 32], P('tp')
- grad_conv_gain: float32 [1536], P('tp')
- grad_out: bfloat16 [1536, 1536], P('tp')
All inputs are finite; a program needn't handle non-finite values.
Results may differ from a plain program's by a relative error of at most 0.027.
Values may be sent and summed in bfloat16 or wider, within the bound.
A program may use at most 64 MiB of HBM per device.

v0:
```python
import jax
import jax.numpy as jnp
from jax import lax
from jax.sharding import PartitionSpec as P

EPS = 1e-05


def with_halo(cells, sides, width):
    for axis, dim in sides:
        count = lax.axis_size(axis)
        ends = count - 1
        head = lax.slice_in_dim(cells, 0, width, axis=dim)
        tail = lax.slice_in_dim(cells, cells.shape[dim] - width, cells.shape[dim], axis=dim)
        cells = jnp.concatenate(
            [
                lax.ppermute(tail, axis, [(i, (i + 1) % count) for i in range(ends)]),
                cells,
                lax.ppermute(head, axis, [((i + 1) % count, i) for i in range(ends)]),
            ],
            axis=dim,
        )
    return cells


def widen(values):
    return lax.optimization_barrier(values).astype(jnp.float32)


def row_sums(values):
    return lax.psum(values, "tp")


def split_norm(values, width):
    mean = row_sums(jnp.sum(values, axis=0, keepdims=True)) / width
    centred = values - mean
    spread = row_sums(jnp.sum(centred * centred, axis=0, keepdims=True)) / width
    inverse = lax.rsqrt(spread + EPS)
    return (centred * inverse, inverse)


def split_norm_back(d_hat, hat, inverse, width):
    first, second = row_sums(
        (jnp.sum(d_hat, axis=0, keepdims=True), jnp.sum(d_hat * hat, axis=0, keepdims=True))
    )
    return (d_hat - first / width - hat * (second / width)) * inverse


def spread_channels(values):
    return lax.all_gather(values, "tp", axis=0, tiled=True)


def frame_rims(values, reach):
    return with_halo(values, (("seq", 1),), reach)


def reduce_inputs(term):
    rounded = widen(term.astype(jnp.bfloat16))
    return lax.psum_scatter(
        rounded.astype(jnp.bfloat16), "tp", scatter_dimension=0, tiled=True
    ).astype(jnp.float32)


def contract_rows(left, right):
    return lax.dot_general(
        left, right, (((0,), (0,)), ((), ())), preferred_element_type=jnp.float32
    )


def contract_cols(left, right):
    return lax.dot_general(
        left, right, (((1,), (1,)), ((), ())), preferred_element_type=jnp.float32
    )


def local(
    frames_in, norm_gain, value_weight, gate_weight, depth_kernel, conv_gain, out_weight, cotangent
):
    chans, row_count = frames_in.shape
    parts = lax.axis_size("tp")
    width = chans * parts
    taps = depth_kernel.shape[1]
    reach = taps // 2
    scale = float(row_count * lax.axis_size("seq")) ** (-0.5)
    inputs = frames_in.astype(jnp.float32)
    hat_in, inverse_in = split_norm(inputs, width)
    normed = (hat_in * norm_gain[:, None]).astype(jnp.bfloat16)
    normed_all = spread_channels(normed)
    value = jnp.dot(value_weight, normed_all, preferred_element_type=jnp.float32)
    gate = jnp.dot(gate_weight, normed_all, preferred_element_type=jnp.float32)
    gate_sig = jax.nn.sigmoid(gate)
    glu = (value * gate_sig).astype(jnp.bfloat16)
    glu_wide = widen(frame_rims(glu, reach))
    conv = jnp.zeros((chans, row_count), jnp.float32)
    for tap in range(taps):
        conv = conv + depth_kernel[:, tap : tap + 1] * glu_wide[:, tap : tap + row_count]
    hat_conv, inverse_conv = split_norm(conv, width)
    scaled = hat_conv * conv_gain[:, None]
    swish_sig = jax.nn.sigmoid(scaled)
    act = (scaled * swish_sig).astype(jnp.bfloat16)
    act_all = spread_channels(act)
    block_out = (inputs + jnp.dot(out_weight, act_all, preferred_element_type=jnp.float32)).astype(
        jnp.bfloat16
    )
    grad_out = contract_cols(cotangent, act_all) * scale
    d_act = reduce_inputs(contract_rows(out_weight, cotangent))
    d_scaled = d_act * (swish_sig + scaled * swish_sig * (1.0 - swish_sig))
    grad_conv_gain = jnp.sum(d_scaled * hat_conv, axis=1) * scale
    d_conv = split_norm_back(d_scaled * conv_gain[:, None], hat_conv, inverse_conv, width).astype(
        jnp.bfloat16
    )
    d_conv_f = widen(d_conv)
    d_conv_wide = widen(frame_rims(d_conv, reach))
    d_glu = jnp.zeros((chans, row_count), jnp.float32)
    kernel_cols = []
    for tap in range(taps):
        start = 2 * reach - tap
        d_glu = d_glu + depth_kernel[:, tap : tap + 1] * d_conv_wide[:, start : start + row_count]
        kernel_cols.append(jnp.sum(glu_wide[:, tap : tap + row_count] * d_conv_f, axis=1))
    grad_kernel = jnp.stack(kernel_cols, axis=1) * scale
    d_value = (d_glu * gate_sig).astype(jnp.bfloat16)
    d_gate = (d_glu * value * gate_sig * (1.0 - gate_sig)).astype(jnp.bfloat16)
    grad_value = contract_cols(d_value, normed_all) * scale
    grad_gate = contract_cols(d_gate, normed_all) * scale
    d_normed = reduce_inputs(
        contract_rows(value_weight, d_value) + contract_rows(gate_weight, d_gate)
    )
    grad_norm_gain = jnp.sum(d_normed * hat_in, axis=1) * scale
    input_grad = (
        cotangent.astype(jnp.float32)
        + split_norm_back(d_normed * norm_gain[:, None], hat_in, inverse_in, width)
    ).astype(jnp.bfloat16)
    grad_out, grad_kernel, grad_conv_gain, grad_value, grad_gate, grad_norm_gain = lax.psum(
        (grad_out, grad_kernel, grad_conv_gain, grad_value, grad_gate, grad_norm_gain), "seq"
    )
    return (
        block_out,
        input_grad,
        grad_norm_gain,
        grad_value.astype(jnp.bfloat16),
        grad_gate.astype(jnp.bfloat16),
        grad_kernel,
        grad_conv_gain,
        grad_out.astype(jnp.bfloat16),
    )


def solution(mesh):
    return jax.shard_map(
        local,
        mesh=mesh,
        in_specs=(
            P("tp", "seq"),
            P("tp"),
            P("tp", None),
            P("tp", None),
            P("tp", None),
            P("tp"),
            P("tp", None),
            P("tp", "seq"),
        ),
        out_specs=(
            P("tp", "seq"),
            P("tp", "seq"),
            P("tp"),
            P("tp", None),
            P("tp", None),
            P("tp", None),
            P("tp"),
            P("tp", None),
        ),
        check_vma=False,
    )
```

profile of v0, /device:TPU:2, one launch (start us, length us, event | category | flops | bytes accessed | tf_op | source)
XLA Modules:
  0.0 620.3 jit_solution(990302388884489150)
XLA Ops:
  7.2 0.0 copy-start
  7.2 0.0 all-gather.3.cloned.1.call-start
  7.2 1.0 convert_reduce_fusion
  8.3 19.2 %psum.98 = f32[1,512]{1,0:T(1,128)S(1)} all-reduce(f32[1,512]{1,0:T(1,128)S(1)} %bitcast.194), channel_id=1, replica_groups=mesh['seq'=64,'tp'=8] {'tp'}, use_global_device_ids=true, to_apply=%region_1.0 | all-reduce | flops 512 | bytes 4096 | tf_op jit(solution)/shard_map/psum | solution.py:31
  27.5 1.0 fusion.21
  28.5 18.0 %psum.99 = f32[1,512]{1,0:T(1,128)S(1)} all-reduce(f32[1,512]{1,0:T(1,128)S(1)} %bitcast.195), channel_id=1, replica_groups=mesh['seq'=64,'tp'=8] {'tp'}, use_global_device_ids=true, to_apply=%region_3.0 | all-reduce | flops 512 | bytes 4096 | tf_op jit(solution)/shard_map/psum | solution.py:31
  46.5 1.7 fusion.16
  48.2 0.0 all-gather.3.cloned.1.call-update
  48.3 0.0 copy-start.13
  48.3 0.0 copy-start.11
  48.3 0.0 reduce-scatter.3.cloned.1.call-start
  48.3 2.9 convolution_convert_fusion
  51.3 0.0 reduce-scatter.3.cloned.1.call-update
  51.3 0.0 all-gather.5.cloned.1.call-start
  51.4 44.4 %all-gather.3.cloned.1.call-done = bf16[1536,512]{1,0:T(8,128)(2,1)} async-done(((bf16[192,512]{1,0:T(8,128)(2,1)}), bf16[1536,512]{1,0:T(8,128)(2,1)}) %all-gather.3.cloned.1.call-update) | async-done | bytes 1572880 | tf_op jit(solution)/shard_map/all_gather | solution.py:50
  95.8 2.1 fusion.6
  97.9 1.2 multiply_convert_fusion.3
  99.1 0.1 fusion.91
  99.2 1.3 collective-permute-start
  100.5 1.3 collective-permute-start.1
  101.9 0.0 copy-start.21
  101.9 0.0 copy-start.22
  101.9 3.6 collective-permute-done.1
  105.5 0.1 pad_maximum_fusion
  105.7 0.0 copy-start.24
  105.7 4.6 fusion.89
  110.4 18.3 %psum.100 = f32[1,512]{1,0:T(1,128)S(1)} all-reduce(f32[1,512]{1,0:T(1,128)S(1)} %bitcast.199), channel_id=1, replica_groups=mesh['seq'=64,'tp'=8] {'tp'}, use_global_device_ids=true, to_apply=%region_5.0 | all-reduce | flops 512 | bytes 4096 | tf_op jit(solution)/shard_map/psum | solution.py:31
  128.8 0.1 multiply_reduce_fusion.2
  128.8 16.7 %psum.101 = f32[1,512]{1,0:T(1,128)S(1)} all-reduce(f32[1,512]{1,0:T(1,128)S(1)} %bitcast.196), channel_id=1, replica_groups=mesh['seq'=64,'tp'=8] {'tp'}, use_global_device_ids=true, to_apply=%region_7.0 | all-reduce | flops 512 | bytes 4096 | tf_op jit(solution)/shard_map/psum | solution.py:31
  145.5 1.7 reduce-scatter.3.cloned.1.call-done
  147.3 2.6 multiply_reduce_fusion
  149.8 18.2 %all-reduce.2 = (f32[1,512]{1,0:T(1,128)S(1)}, f32[1,512]{1,0:T(1,128)S(1)}) all-reduce(f32[1,512]{1,0:T(1,128)S(1)} %bitcast.190, f32[1,512]{1,0:T(1,128)S(1)} %bitcast.191), channel_id=1, replica_groups=mesh['seq'=64,'tp'=8] {'tp'}, use_global_device_ids=true, to_apply=%region_12.0 | all-reduce | flops 1024 | bytes 8192 | tf_op jit(solution)/shard_map/psum | solution.py:31
  168.0 1.9 multiply_convert_fusion.2
  170.0 0.0 all-gather.5.cloned.1.call-update
  170.0 0.0 reduce-scatter.5.cloned.1.call-start
  170.0 0.1 fusion.90
  170.1 1.3 collective-permute-start.2
  171.4 1.5 collective-permute-start.3
  172.9 3.5 collective-permute-done.3
  176.4 0.1 pad_maximum_fusion.1
  176.6 0.0 copy-start.6
  176.6 5.8 multiply_convert_fusion
  182.4 0.1 multiply_convert_fusion.1
  182.5 0.7 fusion.94
  183.2 0.4 copy-done.12
  183.6 1.8 fusion.1
  185.5 0.0 reduce-scatter.5.cloned.1.call-update
  185.5 2.1 fusion.54
  187.6 2.8 fusion.55
  190.3 0.1 stack.131
  190.5 0.6 broadcast_multiply_fusion.7
  191.0 0.6 broadcast_multiply_fusion
  191.6 0.7 convolution_multiply_fusion.1
  192.3 2.7 convolution_multiply_fusion.2
  195.0 22.7 %all-gather.5.cloned.1.call-done = bf16[1536,512]{1,0:T(8,128)(2,1)} async-done(((bf16[192,512]{1,0:T(8,128)(2,1)}), bf16[1536,512]{1,0:T(8,128)(2,1)}) %all-gather.5.cloned.1.call-update) | async-done | bytes 1572880 | tf_op jit(solution)/shard_map/all_gather | solution.py:50
  217.7 3.2 fusion.2
  221.0 1.2 fusion.8
  222.2 46.4 %reduce-scatter.5.cloned.1.call-done = bf16[192,512]{1,0:T(8,128)(2,1)} async-done(((bf16[1536,512]{1,0:T(8,128)(2,1)}), bf16[192,512]{1,0:T(8,128)(2,1)}) %reduce-scatter.5.cloned.1.call-update) | async-done | bytes 196624 | tf_op jit(solution)/shard_map/reduce_scatter | solution.py:59
  268.6 1.1 fusion.23
  269.7 0.6 broadcast_multiply_fusion.8
  270.3 18.3 %all-reduce.1 = (f32[1,512]{1,0:T(1,128)S(1)}, f32[1,512]{1,0:T(1,128)S(1)}) all-reduce(f32[1,512]{1,0:T(1,128)S(1)} %bitcast.192, f32[1,512]{1,0:T(1,128)S(1)} %bitcast.193), channel_id=1, replica_groups=mesh['seq'=64,'tp'=8] {'tp'}, use_global_device_ids=true, to_apply=%region_17.0 | all-reduce | flops 1024 | bytes 8192 | tf_op jit(solution)/shard_map/psum | solution.py:31
  288.7 0.6 broadcast_multiply_fusion.2
  289.3 323.0 %all-reduce.4 = (f32[192]{0:T(256)}, bf16[192,1536]{1,0:T(8,128)(2,1)}, bf16[192,1536]{1,0:T(8,128)(2,1)}, f32[192,32]{0,1:T(8,128)}, f32[192]{0:T(256)}, /*index=5*/bf16[192,1536]{1,0:T(8,128)(2,1)}) all-reduce(f32[192]{0:T(256)} %broadcast_multiply_fusion.8, ...), channel_id=1, replica_groups=mesh['seq'=64,'tp'=8] {'seq'}, use_global_device_ids=true, to_apply=%region_19.0 | all-reduce | flops 891264 | bytes 5360640 | tf_op jit(solution)/shard_map/psum | solution.py:133
  612.3 1.5 fusion.20
  (54 shorter events, 0.3 us)
Async XLA Ops:
  7.2 90.7 %copy-start = (bf16[192,1536]{1,0:T(8,128)(2,1)S(1)}, bf16[192,1536]{1,0:T(8,128)(2,1)}, u32[]{:S(2)}) copy-start(bf16[192,1536]{1,0:T(8,128)(2,1)} %param.10) | copy-start | bytes 1769476
  7.2 88.6 %all-gather.3.cloned.1.call-start = ((), (), s32[]{:S(2)}) async-start(), calls=%async_computation.2 | async-start | bytes 1769472 | tf_op jit(solution)/shard_map/all_gather | solution.py:50
  48.3 3.1 copy-start.13
  48.3 47.5 %copy-start.11 = (bf16[192,1536]{1,0:T(8,128)(2,1)S(1)}, bf16[192,1536]{1,0:T(8,128)(2,1)}, u32[]{:S(2)}) copy-start(bf16[192,1536]{1,0:T(8,128)(2,1)} %param.11) | copy-start | bytes 1769476
  48.3 99.0 %reduce-scatter.3.cloned.1.call-start = ((), (), s32[]{:S(2)}) async-start(), calls=%async_computation.4 | async-start | bytes 1769472 | tf_op jit(solution)/shard_map/reduce_scatter | solution.py:59
  51.3 166.4 %all-gather.5.cloned.1.call-start = ((), (), s32[]{:S(2)}) async-start(), calls=%async_computation.3 | async-start | bytes 1769472 | tf_op jit(solution)/shard_map/all_gather | solution.py:50
  95.8 2.1 copy-start.1
  97.9 1.2 copy-start.5
  99.2 2.7 collective-permute-start
  100.5 5.0 collective-permute-start.1
  101.8 8.5 %copy-start.15 = (f32[192,1]{0,1:T(1,128)}, f32[192,1]{0,1:T(1,128)S(1)}, u32[]{:S(2)}) copy-start(f32[192,1]{0,1:T(1,128)S(1)} %get-tuple-element.91) | copy-start | bytes 2308
  101.8 8.5 %copy-start.16 = (f32[192,1]{0,1:T(1,128)}, f32[192,1]{0,1:T(1,128)S(1)}, u32[]{:S(2)}) copy-start(f32[192,1]{0,1:T(1,128)S(1)} %get-tuple-element.92) | copy-start | bytes 2308
  101.8 8.5 %copy-start.17 = (f32[192,1]{0,1:T(1,128)}, f32[192,1]{0,1:T(1,128)S(1)}, u32[]{:S(2)}) copy-start(f32[192,1]{0,1:T(1,128)S(1)} %get-tuple-element.93) | copy-start | bytes 2308
  101.8 8.5 %copy-start.18 = (f32[192,1]{0,1:T(1,128)}, f32[192,1]{0,1:T(1,128)S(1)}, u32[]{:S(2)}) copy-start(f32[192,1]{0,1:T(1,128)S(1)} %get-tuple-element.94) | copy-start | bytes 2308
  101.9 8.5 %copy-start.19 = (f32[192,1]{0,1:T(1,128)}, f32[192,1]{0,1:T(1,128)S(1)}, u32[]{:S(2)}) copy-start(f32[192,1]{0,1:T(1,128)S(1)} %get-tuple-element.95) | copy-start | bytes 2308
  101.9 8.5 %copy-start.20 = (f32[192,1]{0,1:T(1,128)}, f32[192,1]{0,1:T(1,128)S(1)}, u32[]{:S(2)}) copy-start(f32[192,1]{0,1:T(1,128)S(1)} %get-tuple-element.96) | copy-start | bytes 2308
  101.9 8.5 %copy-start.21 = (f32[192,1]{0,1:T(1,128)}, f32[192,1]{0,1:T(1,128)S(1)}, u32[]{:S(2)}) copy-start(f32[192,1]{0,1:T(1,128)S(1)} %get-tuple-element.97) | copy-start | bytes 2308
  101.9 8.5 %copy-start.22 = (f32[192,1]{0,1:T(1,128)}, f32[192,1]{0,1:T(1,128)S(1)}, u32[]{:S(2)}) copy-start(f32[192,1]{0,1:T(1,128)S(1)} %get-tuple-element.98) | copy-start | bytes 2308
  105.7 41.6 %copy-start.24 = (f32[192]{0:T(256)S(1)}, f32[192]{0:T(256)}, u32[]{:S(2)}) copy-start(f32[192]{0:T(256)} %param.13) | copy-start | bytes 2308
  170.0 98.6 %reduce-scatter.5.cloned.1.call-start = ((), (), s32[]{:S(2)}) async-start(), calls=%async_computation.5 | async-start | bytes 1769472 | tf_op jit(solution)/shard_map/reduce_scatter | solution.py:59
  170.1 2.8 collective-permute-start.2
  171.4 5.0 collective-permute-start.3
  176.6 5.8 copy-start.6
  182.5 0.7 copy-start.9
  182.5 1.1 copy-start.12
  187.6 2.9 copy-start.23
  192.3 25.4 %copy-start.8 = (bf16[192,512]{1,0:T(8,128)(2,1)S(1)}, bf16[192,512]{1,0:T(8,128)(2,1)}, u32[]{:S(2)}) copy-start(bf16[192,512]{1,0:T(8,128)(2,1)} %param.15) | copy-start | bytes 589828
  195.0 26.0 %copy-start.2 = (bf16[192,512]{1,0:T(8,128)(2,1)S(1)}, bf16[192,512]{1,0:T(8,128)(2,1)}, u32[]{:S(2)}) copy-start(bf16[192,512]{1,0:T(8,128)(2,1)} %param.8) | copy-start | bytes 589828
  217.7 3.3 copy-start.3
  217.7 3.3 copy-start.7
  221.0 47.6 %copy-start.14 = (f32[192]{0:T(256)S(1)}, f32[192]{0:T(256)}, u32[]{:S(2)}) copy-start(f32[192]{0:T(256)} %param.9) | copy-start | bytes 2308
  221.0 68.2 %copy-start.4 = (f32[192,1536]{1,0:T(8,128)S(1)}, f32[192,1536]{1,0:T(8,128)}, u32[]{:S(2)}) copy-start(f32[192,1536]{1,0:T(8,128)} %convolution_multiply_fusion.2) | copy-start | bytes 3538948
  289.3 323.0 %copy-start.10 = (bf16[192,512]{1,0:T(8,128)(2,1)S(1)}, bf16[192,512]{1,0:T(8,128)(2,1)}, u32[]{:S(2)}) copy-start(bf16[192,512]{1,0:T(8,128)(2,1)} %reduce-scatter.5.cloned.1.call-done) | copy-start | bytes 589828
Sparse Core Ops, SparseCore 0:
  48.4 47.3 all-gather.2
  98.6 48.5 reduce-scatter.2
  170.1 47.5 all-gather.4
  220.4 48.1 reduce-scatter.4
where the time goes:
time: 621 us; the launch traced here: 620 us
  blocking collectives  432 us (70%)
  waiting for transfers between devices  122 us (20%)
  other arithmetic  29 us (5%)
  matrix products  16.4 us (3%)
  between operations  14.2 us (2%)
    psum x1, blocking collectives, local(): lax.psum((grad_out, grad_kernel, grad_conv_gain, grad_value, grad_gate, g...  323 us
    psum x6, blocking collectives, row_sums(): return lax.psum(values, 'tp')  109 us
    all_gather x2, waiting for transfers between devices, spread_channels(): return lax.all_gather(values, 'tp', axis=0, tiled=True)  67.1 us
    reduce_scatter x2, waiting for transfers between devices, reduce_inputs(): lax.psum_scatter(rounded.astype(jnp.bfloat16), 'tp', scatter_dimension=0,...  48.2 us
  transfers between devices with their start and end apart: 8, of which 6 were waited for; matrix products, arithmetic and copies ran while one was open for 5% of the time, Pallas kernels for 0%

commit v1 on v0

--- a/solution.py
+++ b/solution.py
@@ -47,7 +47,9 @@
 
 
 def spread_channels(values):
-    return lax.all_gather(values, "tp", axis=0, tiled=True)
+    return jnp.concatenate(
+        lax.all_to_all(jnp.stack([values] * lax.axis_size("tp")), "tp", 0, 0), axis=0
+    )
 
 
 def frame_rims(values, reach):

time: 621 us -> 564 us (0.908)
  the two profiles are of different devices: /device:TPU:2 before, /device:TPU:32 now
where the time goes in v1:
time: 564 us; the launch traced here: 563 us
  blocking collectives  427 us (76%)
  waiting for transfers between devices  44.6 us (8%)
  starting transfers between devices  28 us (5%)
  other arithmetic  27.5 us (5%)
  matrix products  15.2 us (3%)
  between operations  14.8 us (3%)
    psum x1, blocking collectives, local(): lax.psum((grad_out, grad_kernel, grad_conv_gain, grad_value, grad_gate, g...  322 us
    psum x6, blocking collectives, row_sums(): return lax.psum(values, 'tp')  106 us
    reduce_scatter x2, waiting for transfers between devices, reduce_inputs(): lax.psum_scatter(rounded.astype(jnp.bfloat16), 'tp', scatter_dimension=0,...  30.8 us
    ppermute x2, starting transfers between devices, with_halo(): lax.ppermute(head, axis, [((i + 1) % count, i) for i in range(ends)])  15.7 us
    all_to_all x2, waiting for transfers between devices, spread_channels(): lax.all_to_all(jnp.stack([values] * lax.axis_size('tp')), 'tp', 0, 0)  12.2 us
  transfers between devices with their start and end apart: 8, of which 4 were waited for; matrix products, arithmetic and copies ran while one was open for 6% of the time, Pallas kernels for 0%

profile of v1, /device:TPU:32, one launch (start us, length us, event | category | flops | bytes accessed | tf_op | source)
XLA Modules:
  0.0 563.0 jit_solution(2144543043569298078)
XLA Ops:
  7.2 0.0 copy-start
  7.2 1.0 convert_reduce_fusion
  8.2 18.9 %psum.98 = f32[1,512]{1,0:T(1,128)S(1)} all-reduce(f32[1,512]{1,0:T(1,128)S(1)} %bitcast.200), channel_id=1, replica_groups=mesh['seq'=64,'tp'=8] {'tp'}, use_global_device_ids=true, to_apply=%region_1.0 | all-reduce | flops 512 | bytes 4096 | tf_op jit(solution)/shard_map/psum | solution.py:31
  27.1 1.0 fusion.21
  28.1 16.1 %psum.99 = f32[1,512]{1,0:T(1,128)S(1)} all-reduce(f32[1,512]{1,0:T(1,128)S(1)} %bitcast.201), channel_id=1, replica_groups=mesh['seq'=64,'tp'=8] {'tp'}, use_global_device_ids=true, to_apply=%region_3.0 | all-reduce | flops 512 | bytes 4096 | tf_op jit(solution)/shard_map/psum | solution.py:31
  44.2 1.0 fusion.16
  45.2 1.3 stack.121
  46.5 3.7 all-to-all-start
  50.2 0.0 copy-start.11
  50.3 0.0 reduce-scatter.3.cloned.1.call-start
  50.3 1.8 convolution_convert_fusion
  52.1 0.0 reduce-scatter.3.cloned.1.call-update
  52.1 0.7 copy-done.13
  52.8 0.7 fusion.92
  53.5 12.2 %all-to-all-done = bf16[8,192,512]{2,1,0:T(8,128)(2,1)S(1)} async-done(((bf16[8,192,512]{2,1,0:T(8,128)(2,1)}), bf16[8,192,512]{2,1,0:T(8,128)(2,1)S(1)}, u32[]{:S(2)}, u32[]{:S(2)}) %all-to-all-start) | async-done | bytes 1572896 | tf_op jit(solution)/shard_map/all_to_all | solution.py:51
  65.7 0.5 fusion.6
  66.2 0.0 copy-start.3
  66.2 1.2 multiply_convert_fusion.3
  67.5 0.0 copy-start.19
  67.6 0.1 fusion.91
  67.7 1.9 collective-permute-start
  69.6 7.9 %collective-permute-start.1 = (bf16[192,16]{1,0:T(8,128)(2,1)S(1)}, bf16[192,16]{1,0:T(8,128)(2,1)S(1)}, u32[]{:S(2)}, u32[]{:S(2)}) collective-permute-start(bf16[192,16]{1,0:T(8,128)(2,1)S(1)} %get-tuple-element.66), channel_id=1, source_target_pairs={{8,0},{16,8},{24,16},{32,24},{40,32},{48,40},{56,48},{64,56},{72,6... | collective-permute-start | bytes 18440 | tf_op jit(solution)/shard_map/ppermute | solution.py:19
  77.6 0.4 collective-permute-done
  78.0 1.2 collective-permute-done.1
  79.3 0.1 pad_maximum_fusion
  79.7 4.6 fusion.89
  84.4 18.4 %psum.100 = f32[1,512]{1,0:T(1,128)S(1)} all-reduce(f32[1,512]{1,0:T(1,128)S(1)} %bitcast.205), channel_id=1, replica_groups=mesh['seq'=64,'tp'=8] {'tp'}, use_global_device_ids=true, to_apply=%region_5.0 | all-reduce | flops 512 | bytes 4096 | tf_op jit(solution)/shard_map/psum | solution.py:31
  102.9 0.1 multiply_reduce_fusion.2
  102.9 16.0 %psum.101 = f32[1,512]{1,0:T(1,128)S(1)} all-reduce(f32[1,512]{1,0:T(1,128)S(1)} %bitcast.202), channel_id=1, replica_groups=mesh['seq'=64,'tp'=8] {'tp'}, use_global_device_ids=true, to_apply=%region_7.0 | all-reduce | flops 512 | bytes 4096 | tf_op jit(solution)/shard_map/psum | solution.py:31
  119.0 0.0 reduce-scatter.3.cloned.1.call-done
  119.0 2.6 multiply_reduce_fusion
  121.6 18.1 %all-reduce.2 = (f32[1,512]{1,0:T(1,128)S(1)}, f32[1,512]{1,0:T(1,128)S(1)}) all-reduce(f32[1,512]{1,0:T(1,128)S(1)} %bitcast.196, f32[1,512]{1,0:T(1,128)S(1)} %bitcast.197), channel_id=1, replica_groups=mesh['seq'=64,'tp'=8] {'tp'}, use_global_device_ids=true, to_apply=%region_12.0 | all-reduce | flops 1024 | bytes 8192 | tf_op jit(solution)/shard_map/psum | solution.py:31
  139.6 1.2 multiply_convert_fusion.2
  140.9 0.1 fusion.90
  141.0 1.9 collective-permute-start.2
  142.9 7.9 %collective-permute-start.3 = (bf16[192,16]{1,0:T(8,128)(2,1)S(1)}, bf16[192,16]{1,0:T(8,128)(2,1)S(1)}, u32[]{:S(2)}, u32[]{:S(2)}) collective-permute-start(bf16[192,16]{1,0:T(8,128)(2,1)S(1)} %get-tuple-element.64), channel_id=1, source_target_pairs={{8,0},{16,8},{24,16},{32,24},{40,32},{48,40},{56,48},{64,56},{72,6... | collective-permute-start | bytes 18440 | tf_op jit(solution)/shard_map/ppermute | solution.py:19
  150.8 1.3 stack.122
  152.0 4.4 all-to-all-start.1
  156.5 0.2 reduce-scatter.5.cloned.1.call-start
  156.7 0.1 pad_maximum_fusion.1
  156.9 5.6 multiply_convert_fusion
  162.5 0.1 multiply_convert_fusion.1
  162.6 0.0 copy-start.9
  162.6 0.7 copy-done.9
  163.3 0.7 fusion.94
  164.0 0.4 copy-done.12
  164.4 1.8 fusion.1
  166.2 0.0 reduce-scatter.5.cloned.1.call-update
  166.2 2.1 fusion.54
  168.3 2.8 fusion.55
  171.0 0.1 stack.155
  171.2 0.6 broadcast_multiply_fusion.7
  171.7 0.6 broadcast_multiply_fusion
  172.3 0.7 convolution_multiply_fusion.1
  173.0 2.7 convolution_multiply_fusion.2
  175.7 3.2 fusion.2
  178.9 2.7 fusion.8
  181.6 30.8 %reduce-scatter.5.cloned.1.call-done = bf16[192,512]{1,0:T(8,128)(2,1)} async-done(((bf16[1536,512]{1,0:T(8,128)(2,1)}), bf16[192,512]{1,0:T(8,128)(2,1)}) %reduce-scatter.5.cloned.1.call-update) | async-done | bytes 196624 | tf_op jit(solution)/shard_map/reduce_scatter | solution.py:61
  212.4 1.1 fusion.23
  213.5 0.6 broadcast_multiply_fusion.8
  214.1 18.0 %all-reduce.1 = (f32[1,512]{1,0:T(1,128)S(1)}, f32[1,512]{1,0:T(1,128)S(1)}) all-reduce(f32[1,512]{1,0:T(1,128)S(1)} %bitcast.198, f32[1,512]{1,0:T(1,128)S(1)} %bitcast.199), channel_id=1, replica_groups=mesh['seq'=64,'tp'=8] {'tp'}, use_global_device_ids=true, to_apply=%region_17.0 | all-reduce | flops 1024 | bytes 8192 | tf_op jit(solution)/shard_map/psum | solution.py:31
  232.1 0.6 broadcast_multiply_fusion.2
  232.7 321.9 %all-reduce.4 = (f32[192]{0:T(256)}, bf16[192,1536]{1,0:T(8,128)(2,1)}, bf16[192,1536]{1,0:T(8,128)(2,1)}, f32[192,32]{0,1:T(8,128)}, f32[192]{0:T(256)}, /*index=5*/bf16[192,1536]{1,0:T(8,128)(2,1)}) all-reduce(f32[192]{0:T(256)} %broadcast_multiply_fusion.8, ...), channel_id=1, replica_groups=mesh['seq'=64,'tp'=8] {'seq'}, use_global_device_ids=true, to_apply=%region_19.0 | all-reduce | flops 891264 | bytes 5360640 | tf_op jit(solution)/shard_map/psum | solution.py:135
  554.6 1.5 fusion.20
  (98 shorter events, 0.3 us)
Async XLA Ops:
  7.2 59.0 %copy-start = (bf16[192,1536]{1,0:T(8,128)(2,1)S(1)}, bf16[192,1536]{1,0:T(8,128)(2,1)}, u32[]{:S(2)}) copy-start(bf16[192,1536]{1,0:T(8,128)(2,1)} %param.10) | copy-start | bytes 1769476
  46.5 3.8 copy-start.5
  46.5 3.8 copy-start.7
  46.5 19.1 %all-to-all-start = ((bf16[8,192,512]{2,1,0:T(8,128)(2,1)}), bf16[8,192,512]{2,1,0:T(8,128)(2,1)S(1)}, u32[]{:S(2)}, u32[]{:S(2)}) async-start(bf16[8,192,512]{2,1,0:T(8,128)(2,1)} %stack.121), calls=%async_computation | async-start | bytes 3145728 | tf_op jit(solution)/shard_map/all_to_all | solution.py:51
  50.2 15.4 %copy-start.11 = (bf16[192,1536]{1,0:T(8,128)(2,1)S(1)}, bf16[192,1536]{1,0:T(8,128)(2,1)}, u32[]{:S(2)}) copy-start(bf16[192,1536]{1,0:T(8,128)(2,1)} %param.11) | copy-start | bytes 1769476
  50.3 68.7 %reduce-scatter.3.cloned.1.call-start = ((), (), s32[]{:S(2)}) async-start(), calls=%async_computation.4 | async-start | bytes 1769472 | tf_op jit(solution)/shard_map/reduce_scatter | solution.py:61
  52.1 0.8 copy-start.13
  66.2 1.4 copy-start.3
  67.4 12.0 %copy-start.15 = (f32[192,1]{0,1:T(1,128)S(1)}, f32[192,1]{0,1:T(1,128)}, u32[]{:S(2)}) copy-start(f32[192,1]{0,1:T(1,128)} %get-tuple-element.69) | copy-start | bytes 2308
  67.4 12.0 %copy-start.16 = (f32[192,1]{0,1:T(1,128)S(1)}, f32[192,1]{0,1:T(1,128)}, u32[]{:S(2)}) copy-start(f32[192,1]{0,1:T(1,128)} %get-tuple-element.70) | copy-start | bytes 2308
  67.4 12.0 %copy-start.17 = (f32[192,1]{0,1:T(1,128)S(1)}, f32[192,1]{0,1:T(1,128)}, u32[]{:S(2)}) copy-start(f32[192,1]{0,1:T(1,128)} %get-tuple-element.71) | copy-start | bytes 2308
  67.4 12.1 %copy-start.18 = (f32[192,1]{0,1:T(1,128)S(1)}, f32[192,1]{0,1:T(1,128)}, u32[]{:S(2)}) copy-start(f32[192,1]{0,1:T(1,128)} %get-tuple-element.72) | copy-start | bytes 2308
  67.5 12.1 %copy-start.19 = (f32[192,1]{0,1:T(1,128)S(1)}, f32[192,1]{0,1:T(1,128)}, u32[]{:S(2)}) copy-start(f32[192,1]{0,1:T(1,128)} %get-tuple-element.73) | copy-start | bytes 2308
  67.5 12.1 %copy-start.20 = (f32[192,1]{0,1:T(1,128)S(1)}, f32[192,1]{0,1:T(1,128)}, u32[]{:S(2)}) copy-start(f32[192,1]{0,1:T(1,128)} %get-tuple-element.74) | copy-start | bytes 2308
  67.5 12.1 %copy-start.21 = (f32[192,1]{0,1:T(1,128)S(1)}, f32[192,1]{0,1:T(1,128)}, u32[]{:S(2)}) copy-start(f32[192,1]{0,1:T(1,128)} %get-tuple-element.75) | copy-start | bytes 2308
  67.5 12.1 %copy-start.22 = (f32[192,1]{0,1:T(1,128)S(1)}, f32[192,1]{0,1:T(1,128)}, u32[]{:S(2)}) copy-start(f32[192,1]{0,1:T(1,128)} %get-tuple-element.76) | copy-start | bytes 2308
  67.5 12.1 %copy-start.23 = (f32[192,1]{0,1:T(1,128)S(1)}, f32[192,1]{0,1:T(1,128)}, u32[]{:S(2)}) copy-start(f32[192,1]{0,1:T(1,128)} %get-tuple-element.77) | copy-start | bytes 2308
  67.5 12.1 %copy-start.24 = (f32[192,1]{0,1:T(1,128)S(1)}, f32[192,1]{0,1:T(1,128)}, u32[]{:S(2)}) copy-start(f32[192,1]{0,1:T(1,128)} %get-tuple-element.78) | copy-start | bytes 2308
  67.5 12.1 %copy-start.25 = (f32[192,1]{0,1:T(1,128)S(1)}, f32[192,1]{0,1:T(1,128)}, u32[]{:S(2)}) copy-start(f32[192,1]{0,1:T(1,128)} %get-tuple-element.79) | copy-start | bytes 2308
  67.5 12.1 %copy-start.26 = (f32[192,1]{0,1:T(1,128)S(1)}, f32[192,1]{0,1:T(1,128)}, u32[]{:S(2)}) copy-start(f32[192,1]{0,1:T(1,128)} %get-tuple-element.80) | copy-start | bytes 2308
  67.5 12.1 %copy-start.27 = (f32[192,1]{0,1:T(1,128)S(1)}, f32[192,1]{0,1:T(1,128)}, u32[]{:S(2)}) copy-start(f32[192,1]{0,1:T(1,128)} %get-tuple-element.81) | copy-start | bytes 2308
  67.5 12.1 %copy-start.28 = (f32[192,1]{0,1:T(1,128)S(1)}, f32[192,1]{0,1:T(1,128)}, u32[]{:S(2)}) copy-start(f32[192,1]{0,1:T(1,128)} %get-tuple-element.82) | copy-start | bytes 2308
  67.6 12.1 %copy-start.29 = (f32[192,1]{0,1:T(1,128)S(1)}, f32[192,1]{0,1:T(1,128)}, u32[]{:S(2)}) copy-start(f32[192,1]{0,1:T(1,128)} %get-tuple-element.83) | copy-start | bytes 2308
  67.6 12.1 %copy-start.30 = (f32[192,1]{0,1:T(1,128)S(1)}, f32[192,1]{0,1:T(1,128)}, u32[]{:S(2)}) copy-start(f32[192,1]{0,1:T(1,128)} %get-tuple-element.84) | copy-start | bytes 2308
  67.6 12.1 %copy-start.31 = (f32[192,1]{0,1:T(1,128)S(1)}, f32[192,1]{0,1:T(1,128)}, u32[]{:S(2)}) copy-start(f32[192,1]{0,1:T(1,128)} %get-tuple-element.85) | copy-start | bytes 2308
  67.7 10.4 %collective-permute-start = (bf16[192,16]{1,0:T(8,128)(2,1)S(1)}, bf16[192,16]{1,0:T(8,128)(2,1)S(1)}, u32[]{:S(2)}, u32[]{:S(2)}) collective-permute-start(bf16[192,16]{1,0:T(8,128)(2,1)S(1)} %get-tuple-element.65), channel_id=1, source_target_pairs={{0,8},{8,16},{16,24},{24,32},{32,40},{40,48},{48,56},{56,64},{64,7... | collective-permute-start | bytes 18440 | tf_op jit(solution)/shard_map/ppermute | solution.py:17
  69.6 9.7 %collective-permute-start.1 = (bf16[192,16]{1,0:T(8,128)(2,1)S(1)}, bf16[192,16]{1,0:T(8,128)(2,1)S(1)}, u32[]{:S(2)}, u32[]{:S(2)}) collective-permute-start(bf16[192,16]{1,0:T(8,128)(2,1)S(1)} %get-tuple-element.66), channel_id=1, source_target_pairs={{8,0},{16,8},{24,16},{32,24},{40,32},{48,40},{56,48},{64,56},{72,6... | collective-permute-start | bytes 18440 | tf_op jit(solution)/shard_map/ppermute | solution.py:19
  77.5 6.8 %copy-start.32 = (f32[192,1]{0,1:T(1,128)}, f32[192,1]{0,1:T(1,128)S(1)}, u32[]{:S(2)}) copy-start(f32[192,1]{0,1:T(1,128)S(1)} %get-tuple-element.86) | copy-start | bytes 2308
  77.5 6.8 %copy-start.33 = (f32[192,1]{0,1:T(1,128)}, f32[192,1]{0,1:T(1,128)S(1)}, u32[]{:S(2)}) copy-start(f32[192,1]{0,1:T(1,128)S(1)} %get-tuple-element.87) | copy-start | bytes 2308
  77.5 6.8 %copy-start.34 = (f32[192,1]{0,1:T(1,128)}, f32[192,1]{0,1:T(1,128)S(1)}, u32[]{:S(2)}) copy-start(f32[192,1]{0,1:T(1,128)S(1)} %get-tuple-element.88) | copy-start | bytes 2308
  77.5 6.8 %copy-start.35 = (f32[192,1]{0,1:T(1,128)}, f32[192,1]{0,1:T(1,128)S(1)}, u32[]{:S(2)}) copy-start(f32[192,1]{0,1:T(1,128)S(1)} %get-tuple-element.89) | copy-start | bytes 2308
  77.5 6.8 %copy-start.36 = (f32[192,1]{0,1:T(1,128)}, f32[192,1]{0,1:T(1,128)S(1)}, u32[]{:S(2)}) copy-start(f32[192,1]{0,1:T(1,128)S(1)} %get-tuple-element.90) | copy-start | bytes 2308
  77.5 6.8 %copy-start.37 = (f32[192,1]{0,1:T(1,128)}, f32[192,1]{0,1:T(1,128)S(1)}, u32[]{:S(2)}) copy-start(f32[192,1]{0,1:T(1,128)S(1)} %get-tuple-element.91) | copy-start | bytes 2308
  77.6 6.8 %copy-start.38 = (f32[192,1]{0,1:T(1,128)}, f32[192,1]{0,1:T(1,128)S(1)}, u32[]{:S(2)}) copy-start(f32[192,1]{0,1:T(1,128)S(1)} %get-tuple-element.92) | copy-start | bytes 2308
  77.6 6.8 %copy-start.39 = (f32[192,1]{0,1:T(1,128)}, f32[192,1]{0,1:T(1,128)S(1)}, u32[]{:S(2)}) copy-start(f32[192,1]{0,1:T(1,128)S(1)} %get-tuple-element.93) | copy-start | bytes 2308
  77.6 6.8 %copy-start.40 = (f32[192,1]{0,1:T(1,128)}, f32[192,1]{0,1:T(1,128)S(1)}, u32[]{:S(2)}) copy-start(f32[192,1]{0,1:T(1,128)S(1)} %get-tuple-element.94) | copy-start | bytes 2308
  77.6 6.8 %copy-start.41 = (f32[192,1]{0,1:T(1,128)}, f32[192,1]{0,1:T(1,128)S(1)}, u32[]{:S(2)}) copy-start(f32[192,1]{0,1:T(1,128)S(1)} %get-tuple-element.95) | copy-start | bytes 2308
  77.6 6.8 %copy-start.42 = (f32[192,1]{0,1:T(1,128)}, f32[192,1]{0,1:T(1,128)S(1)}, u32[]{:S(2)}) copy-start(f32[192,1]{0,1:T(1,128)S(1)} %get-tuple-element.96) | copy-start | bytes 2308
  77.6 6.8 %copy-start.43 = (f32[192,1]{0,1:T(1,128)}, f32[192,1]{0,1:T(1,128)S(1)}, u32[]{:S(2)}) copy-start(f32[192,1]{0,1:T(1,128)S(1)} %get-tuple-element.97) | copy-start | bytes 2308
  77.6 6.8 %copy-start.44 = (f32[192,1]{0,1:T(1,128)}, f32[192,1]{0,1:T(1,128)S(1)}, u32[]{:S(2)}) copy-start(f32[192,1]{0,1:T(1,128)S(1)} %get-tuple-element.98) | copy-start | bytes 2308
  79.6 39.4 %copy-start.46 = (f32[192]{0:T(256)S(1)}, f32[192]{0:T(256)}, u32[]{:S(2)}) copy-start(f32[192]{0:T(256)} %param.13) | copy-start | bytes 2308
  141.0 15.7 %collective-permute-start.2 = (bf16[192,16]{1,0:T(8,128)(2,1)S(1)}, bf16[192,16]{1,0:T(8,128)(2,1)S(1)}, u32[]{:S(2)}, u32[]{:S(2)}) collective-permute-start(bf16[192,16]{1,0:T(8,128)(2,1)S(1)} %get-tuple-element.63), channel_id=1, source_target_pairs={{0,8},{8,16},{16,24},{24,32},{32,40},{40,48},{48,56},{56,64},{64,7... | collective-permute-start | bytes 18440 | tf_op jit(solution)/shard_map/ppermute | solution.py:17
  142.9 13.8 %collective-permute-start.3 = (bf16[192,16]{1,0:T(8,128)(2,1)S(1)}, bf16[192,16]{1,0:T(8,128)(2,1)S(1)}, u32[]{:S(2)}, u32[]{:S(2)}) collective-permute-start(bf16[192,16]{1,0:T(8,128)(2,1)S(1)} %get-tuple-element.64), channel_id=1, source_target_pairs={{8,0},{16,8},{24,16},{32,24},{40,32},{48,40},{56,48},{64,56},{72,6... | collective-permute-start | bytes 18440 | tf_op jit(solution)/shard_map/ppermute | solution.py:19
  152.0 4.9 copy-start.4
  152.0 23.7 %all-to-all-start.1 = ((bf16[8,192,512]{2,1,0:T(8,128)(2,1)}), bf16[8,192,512]{2,1,0:T(8,128)(2,1)}, u32[]{:S(2)}, u32[]{:S(2)}) async-start(bf16[8,192,512]{2,1,0:T(8,128)(2,1)} %stack.122), calls=%async_computation.1 | async-start | bytes 3145728 | tf_op jit(solution)/shard_map/all_to_all | solution.py:51
  156.5 55.9 %reduce-scatter.5.cloned.1.call-start = ((), (), s32[]{:S(2)}) async-start(), calls=%async_computation.5 | async-start | bytes 1769472 | tf_op jit(solution)/shard_map/reduce_scatter | solution.py:61
  162.6 0.7 copy-start.9
  163.3 1.1 copy-start.12
  168.3 2.9 copy-start.45
  173.0 2.7 copy-start.8
  175.7 3.2 copy-start.1
  175.7 3.2 copy-start.6
  178.9 33.5 %copy-start.14 = (f32[192]{0:T(256)S(1)}, f32[192]{0:T(256)}, u32[]{:S(2)}) copy-start(f32[192]{0:T(256)} %param.9) | copy-start | bytes 2308
  178.9 53.8 %copy-start.2 = (f32[192,1536]{1,0:T(8,128)S(1)}, f32[192,1536]{1,0:T(8,128)}, u32[]{:S(2)}) copy-start(f32[192,1536]{1,0:T(8,128)} %convolution_multiply_fusion.2) | copy-start | bytes 3538948
  232.7 321.9 %copy-start.10 = (bf16[192,512]{1,0:T(8,128)(2,1)S(1)}, bf16[192,512]{1,0:T(8,128)(2,1)}, u32[]{:S(2)}) copy-start(bf16[192,512]{1,0:T(8,128)(2,1)} %reduce-scatter.5.cloned.1.call-done) | copy-start | bytes 589828
Sparse Core Ops, SparseCore 0:
  53.9 54.9 reduce-scatter.2
  166.3 46.0 reduce-scatter.4
